TPU v7x, 32 devices: a whole 2x2x4 slice. The times are simulated.
32 devices in a mesh: grp: 4 (over z), aux: 8 (over y, x, core).
Axes of the slice: x: 2, y: 2, z: 4, core: 2. Of those that a mesh axis runs over, the one named last changes fastest.
Arguments:
- integrals: bfloat16 [2048, 16384], P('aux', 'grp'), parts along dimension 1, may hold values from -6 to 6
- inverses: bfloat16 [4, 512, 512], P(None, 'aux'), as said below
- lower_blocks: bfloat16 [6, 512, 512], P(None, 'aux'), may hold values from -0.25 to 0.25
Outputs:
- solved: bfloat16 [2048, 16384], P(None, ('grp', 'aux')), parts along dimension 1
There are 4 independent parts, one for each index of `grp`. A program takes and returns all parts, laid end to end along the dimension named above; an argument that names none is the same for every part. Nothing has to cross between parts.
Inputs may be any that keep to these rules, and one draw needn't show every extreme that they name: Each inverses[k] is lower triangular with diagonal entries between 0.5 and 1.5.
All inputs are finite; a program needn't handle non-finite values.
Results may differ from a plain program's by a relative error of at most 0.007.
Values may be sent and summed in bfloat16 or wider, within the bound.
A program may use at most 64 MiB of HBM per device.

v0:
```python
import jax
import jax.numpy as jnp
from jax import lax
from jax.sharding import PartitionSpec as P


def local(integrals, inverses, lower_blocks):
    inv_all, low_all = (
        lax.all_gather(inverses, "aux", axis=1, tiled=True),
        lax.all_gather(lower_blocks, "aux", axis=1, tiled=True),
    )
    count = inv_all.shape[0]
    panel = inv_all.shape[1]
    width = integrals.shape[0]
    groups = lax.axis_size("aux")
    rows = integrals.shape[1] // groups
    sectioned = integrals.reshape(width, groups, rows)
    block = lax.all_to_all(sectioned, "aux", split_axis=1, concat_axis=0, tiled=True)
    columns = block.reshape(block.shape[0], block.shape[2])
    outs = []
    for k in range(count):
        acc = columns[k * panel : (k + 1) * panel].astype(jnp.float32)
        for j in range(k):
            acc = acc - jnp.dot(
                low_all[k * (k - 1) // 2 + j], outs[j], preferred_element_type=jnp.float32
            )
        rest = acc.astype(jnp.bfloat16)
        outs.append(
            jnp.dot(inv_all[k], rest, preferred_element_type=jnp.float32).astype(jnp.bfloat16)
        )
    return jnp.concatenate(outs, axis=0)


def solution(mesh):
    placed = (P("aux", "grp"), P(None, "aux", None), P(None, "aux", None))
    return jax.shard_map(
        local, mesh=mesh, in_specs=placed, out_specs=P(None, ("grp", "aux")), check_vma=False
    )
```

profile of v0, /device:TPU:0, one launch (start us, length us, event | category | flops | bytes accessed | tf_op | source)
XLA Modules:
  0.0 108.9 jit_solution(14230477179724768061)
XLA Ops:
  6.5 0.0 all-gather.3.cloned.1.call-start
  6.5 0.7 all-gather.3.cloned.1.call-update
  7.3 0.0 all-gather.5.cloned.1.call-start
  7.3 0.7 all-gather.5.cloned.1.call-update
  8.0 3.3 %copy.4 = bf16[256,4096]{0,1:T(8,128)(2,1)S(1)} copy(bf16[256,4096]{1,0:T(8,128)(2,1)} %param.3) | data formatting | bytes 4194304 | tf_op args[0]
  11.3 40.0 %all_to_all.15 = bf16[256,8,512]{0,2,1:T(8,128)(2,1)S(1)} all-to-all(bf16[256,8,512]{0,2,1:T(8,128)(2,1)S(1)} %bitcast.90), channel_id=1, replica_groups=mesh['grp'=4,'aux'=8] {'aux'}, dimensions={1} | all-to-all | bytes 4194304 | tf_op jit(solution)/shard_map/all_to_all | solution.py:18
  51.3 1.3 %slice_convert_fusion.1 = (f32[2,256,1,512]{1,3,0,2:T(8,128)}, f32[2,256,1,512]{1,3,0,2:T(8,128)S(1)}, f32[2,256,1,512]{1,3,0,2:T(8,128)S(1)}, bf16[2,256,1,512]{1,3,0,2:T(8,128)(2,1)S(1)}) fusion(bf16[8,256,1,512]{1,3,0,2:T(8,128)(2,1)S(1)} %bitcast.91), kind=kLoop, calls=%fused_computation.29 | loop fusion | flops 786432 | bytes 5767168 | tf_op jit(solution)/shard_map/convert_element_type | solution.py:22
  52.5 1.0 copy.5
  53.6 0.3 copy.6
  53.9 1.3 %copy.7 = f32[512,512]{0,1:T(8,128)} copy(f32[512,512]{1,0:T(8,128)S(1)} %bitcast.92) | data formatting | bytes 2097152 | tf_op jit(solution)/shard_map/convert_element_type | solution.py:22
  55.3 1.6 %copy.8 = f32[2,256,1,512]{3,1,0,2:T(8,128)S(1)} copy(f32[2,256,1,512]{1,3,0,2:T(8,128)} %get-tuple-element.5) | data formatting | bytes 2097152 | tf_op jit(solution)/shard_map/convert_element_type | solution.py:22
  56.8 0.3 copy.9
  57.2 1.3 %copy.10 = f32[2,256,1,512]{3,1,0,2:T(8,128)} copy(f32[2,256,1,512]{1,3,0,2:T(8,128)S(1)} %get-tuple-element.6) | data formatting | bytes 2097152 | tf_op jit(solution)/shard_map/convert_element_type | solution.py:22
  58.5 1.6 %copy.11 = f32[512,512]{0,1:T(8,128)S(1)} copy(f32[512,512]{1,0:T(8,128)} %bitcast.94) | data formatting | bytes 2097152 | tf_op jit(solution)/shard_map/convert_element_type | solution.py:22
  60.0 0.0 all-gather.3.cloned.1.call-done
  60.1 1.7 %convolution_convert_fusion.3 = bf16[512,512]{1,0:T(8,128)(2,1)S(1)} fusion(bf16[512,512]{1,0:T(8,128)(2,1)} %bitcast.96, bf16[4,512,512]{2,1,0:T(8,128)(2,1)} %all-gather.3.cloned.1.call-done), kind=kOutput, calls=%fused_computation.16 | convolution fusion | flops 268697600 | bytes 1572864 | tf_op jit(solution)/shard_map/dot_general | solution.py:29
  61.7 24.6 %all-gather.5.cloned.1.call-done = bf16[6,512,512]{2,1,0:T(8,128)(2,1)} async-done(((bf16[6,64,512]{2,1,0:T(8,128)(2,1)}), bf16[6,512,512]{2,1,0:T(8,128)(2,1)}) %all-gather.5.cloned.1.call-update) | async-done | bytes 3145744 | tf_op jit(solution)/shard_map/all_gather | solution.py:10
  86.3 3.2 %convolution_convert_fusion.2 = bf16[512,512]{0,1:T(8,128)(2,1)} fusion(f32[512,512]{0,1:T(8,128)} %copy.7, bf16[512,512]{1,0:T(8,128)(2,1)S(1)} %convolution_convert_fusion.3, bf16[4,512,512]{2,1,0:T(8,128)(2,1)} %all-gather.3.cloned.1.call-done, bf16[6,512,512]{2,1,0:T(8,128)(2,1)} %all-gather.5.cloned.1.call-done), kind=kOutput, calls=%fused_computation.15 | convolution fusion | flops 537657344 | bytes 3145728 | tf_op jit(solution)/shard_map/dot_general | solution.py:29
  89.5 2.5 %fusion.4 = f32[512,512]{0,1:T(8,128)} fusion(f32[512,512]{0,1:T(8,128)S(1)} %copy.9, bf16[512,512]{1,0:T(8,128)(2,1)S(1)} %convolution_convert_fusion.3, bf16[6,512,512]{2,1,0:T(8,128)(2,1)} %all-gather.5.cloned.1.call-done), kind=kOutput, calls=%fused_computation.10 | convolution fusion | flops 268697600 | bytes 3145728 | tf_op jit(solution)/shard_map/dot_general | solution.py:24
  92.0 0.0 copy-start
  92.0 1.6 %fusion.2 = f32[512,512]{0,1:T(8,128)S(1)} fusion(f32[512,512]{0,1:T(8,128)S(1)} %copy.11, bf16[512,512]{1,0:T(8,128)(2,1)S(1)} %convolution_convert_fusion.3, bf16[6,512,512]{2,1,0:T(8,128)(2,1)} %all-gather.5.cloned.1.call-done), kind=kOutput, calls=%fused_computation.6 | convolution fusion | flops 268697600 | bytes 3145728 | tf_op jit(solution)/shard_map/dot_general | solution.py:24
  93.6 0.0 copy-done
  93.6 3.2 %convolution_convert_fusion.1 = bf16[512,512]{0,1:T(8,128)(2,1)} fusion(f32[512,512]{0,1:T(8,128)} %fusion.4, bf16[512,512]{0,1:T(8,128)(2,1)S(1)} %copy-done, bf16[4,512,512]{2,1,0:T(8,128)(2,1)} %all-gather.3.cloned.1.call-done, bf16[6,512,512]{2,1,0:T(8,128)(2,1)} %all-gather.5.cloned.1.call-done), kind=kOutput, calls=%fused_computation.14 | convolution fusion | flops 537657344 | bytes 3145728 | tf_op jit(solution)/shard_map/dot_general | solution.py:29
  96.8 1.5 %fusion.1 = f32[512,512]{0,1:T(8,128)S(1)} fusion(f32[512,512]{0,1:T(8,128)S(1)} %fusion.2, bf16[512,512]{0,1:T(8,128)(2,1)S(1)} %copy-done, bf16[6,512,512]{2,1,0:T(8,128)(2,1)} %all-gather.5.cloned.1.call-done), kind=kOutput, calls=%fused_computation.4 | convolution fusion | flops 268697600 | bytes 3145728 | tf_op jit(solution)/shard_map/dot_general | solution.py:24
  98.3 0.0 copy-start.1
  98.4 2.3 %fusion.9 = bf16[512,512]{1,0:T(8,128)(2,1)S(1)} fusion(f32[512,512]{0,1:T(8,128)S(1)} %fusion.1, bf16[512,512]{0,1:T(8,128)(2,1)} %convolution_convert_fusion.1, bf16[4,512,512]{2,1,0:T(8,128)(2,1)} %all-gather.3.cloned.1.call-done, bf16[6,512,512]{2,1,0:T(8,128)(2,1)} %all-gather.5.cloned.1.call-done), kind=kOutput, calls=%fused_computation.20 | convolution fusion | flops 537657344 | bytes 3145728 | tf_op jit(solution)/shard_map/dot_general | solution.py:29
  100.6 0.0 copy-done.1
  100.6 1.5 %pad_maximum_fusion = bf16[2048,512]{1,0:T(8,128)(2,1)} fusion(bf16[512,512]{1,0:T(8,128)(2,1)S(1)} %fusion.9, bf16[512,512]{1,0:T(8,128)(2,1)S(1)} %bitcast.97, bf16[512,512]{1,0:T(8,128)(2,1)S(1)} %bitcast.95, bf16[512,512]{1,0:T(8,128)(2,1)S(1)} %convolution_convert_fusion.3), kind=kLoop, calls=%fused_computation | loop fusion | flops 8388608 | bytes 4194304 | tf_op jit(solution)/shard_map/concatenate | solution.py:31
Async XLA Ops:
  6.5 53.5 %all-gather.3.cloned.1.call-start = ((), (), s32[]{:S(2)}) async-start(), calls=%async_computation.1 | async-start | bytes 2359296 | tf_op jit(solution)/shard_map/all_gather | solution.py:9
  7.3 79.1 %all-gather.5.cloned.1.call-start = ((), (), s32[]{:S(2)}) async-start(), calls=%async_computation.2 | async-start | bytes 3538944 | tf_op jit(solution)/shard_map/all_gather | solution.py:10
  92.0 1.6 %copy-start = (bf16[512,512]{0,1:T(8,128)(2,1)S(1)}, bf16[512,512]{0,1:T(8,128)(2,1)}, u32[]{:S(2)}) copy-start(bf16[512,512]{0,1:T(8,128)(2,1)} %convolution_convert_fusion.2) | copy-start | bytes 1572868
  98.3 2.3 %copy-start.1 = (bf16[512,512]{0,1:T(8,128)(2,1)S(1)}, bf16[512,512]{0,1:T(8,128)(2,1)}, u32[]{:S(2)}) copy-start(bf16[512,512]{0,1:T(8,128)(2,1)} %convolution_convert_fusion.1) | copy-start | bytes 1572868
Sparse Core Ops, SparseCore 0:
  9.2 41.8 all-gather.2
  53.0 33.2 all-gather.4
where the time goes:
time: 109 us
  blocking collectives  40 us (37%)
  waiting for transfers between devices  26 us (24%)
  matrix products  15.9 us (15%)
  between operations  13.5 us (12%)
  local copies, waits for them, and re-layouts  10.7 us (10%)
  other arithmetic  2.73 us (3%)
    all_to_all x1, blocking collectives, local(): lax.all_to_all(sectioned, 'aux', split_axis=1, concat_axis=0, tiled=True)  40 us
    all_gather x1, waiting for transfers between devices, local(): lax.all_gather(lower_blocks, 'aux', axis=1, tiled=True)  24.6 us
    dot_general x4, matrix products, local(): jnp.dot(inv_all[k], rest, preferred_element_type=jnp.float32)  10.3 us
    convert_element_type x6, local copies, waits for them, and re-layouts, local(): acc = columns[k * panel:(k + 1) * panel].astype(jnp.float32)  6.43 us
    dot_general x3, matrix products, local(): jnp.dot(low_all[k * (k - 1) // 2 + j], outs[j], preferred_element_type=jn...  5.61 us
    unnamed x5, local copies, waits for them, and re-layouts  3.28 us
  transfers between devices with their start and end apart: 2, of which 1 were waited for; matrix products, arithmetic and copies ran while one was open for 13% of the time, Pallas kernels for 0%

commit v1 on v0

v1 whole, which is shorter than its diff:
```python
import functools

import jax
import jax.numpy as jnp
from jax import lax
from jax.experimental import pallas as pl
from jax.experimental.pallas import tpu as pltpu
from jax.sharding import PartitionSpec as P

MESH = pl.DeviceIdType.MESH
PARTS = 2


def flip(index, offset):
    result = 0
    bit = 1
    while bit <= offset or bit == 1:
        if offset & bit:
            result = result + bit * ((index // bit + 1) % 2)
        else:
            result = result + bit * ((index // bit) % 2)
        bit *= 2
    return result + (index // bit) * bit


def kernel(n, pair, x_ref, inv_ref, low_ref, out_ref, cols, inv_all, low_all,
           a2a_send, a2a_recv, fac_send, fac_recv, own_send, own_recv, local_sem):
    me = lax.axis_index("aux")
    group = lax.axis_index("grp")
    held = x_ref.shape[0]
    width = out_ref.shape[1]
    part = width // PARTS
    count, rows, panel = inv_ref.shape
    mate = flip(me, 1)
    halves = 2 if pair else 1
    half = group % 2 if pair else 0
    other = (group + 1) % 2
    twin = flip(group, 1)

    def at(device):
        return pl.ds(pl.multiple_of(device * rows, rows), rows)

    locals_ = []
    mine = pl.ds(pl.multiple_of(me * held, held), held)
    for h in range(PARTS):
        locals_.append(pltpu.make_async_copy(
            x_ref.at[:, pl.ds(pl.multiple_of(me * width + h * part, part), part)],
            cols.at[mine, pl.ds(h * part, part)],
            local_sem.at[h]))
    locals_.append(pltpu.make_async_copy(inv_ref, inv_all.at[:, at(me)], local_sem.at[PARTS]))
    locals_.append(pltpu.make_async_copy(low_ref, low_all.at[:, at(me)], local_sem.at[PARTS + 1]))
    for copy in locals_:
        copy.start()

    barrier = pltpu.get_barrier_semaphore()
    for o in range(1, n):
        pl.semaphore_signal(barrier, inc=1, device_id={"aux": flip(me, o)}, device_id_type=MESH)
    if pair:
        pl.semaphore_signal(barrier, inc=1, device_id={"grp": twin}, device_id_type=MESH)
    pl.semaphore_wait(barrier, n if pair else n - 1)

    steps = [o for o in range(2, n, 2)]

    def blocks(ref, which):
        size = ref.shape[0] // halves
        return pl.ds(which * size, size)

    def factor(kind, slot, which, owner, target, first=False):
        copies = []
        for i, (src, dst) in enumerate(((inv_ref, inv_all), (low_ref, low_all))):
            place = dst.at[blocks(dst, which), at(owner)]
            copies.append(pltpu.make_async_remote_copy(
                src_ref=src.at[blocks(src, which)] if first else place,
                dst_ref=place,
                send_sem=fac_send.at[kind, slot, i],
                recv_sem=fac_recv.at[kind, slot, i],
                device_id=target,
                device_id_type=MESH))
        return copies

    def start(copies):
        for copy in copies:
            copy.start()
        return copies

    pending = []
    gather = [start(factor(0, s, half, me, {"aux": flip(me, o)}, True)) for s, o in enumerate(steps)]
    own = []
    for i, (src, dst) in enumerate(((inv_ref, inv_all), (low_ref, low_all))):
        own.append(pltpu.make_async_remote_copy(
            src_ref=src, dst_ref=dst.at[:, at(me)],
            send_sem=own_send.at[i], recv_sem=own_recv.at[i],
            device_id={"aux": mate}, device_id_type=MESH))
    start(own)

    order = sorted(range(1, n), key=lambda o: (-(o % 2 == 0), -o))
    order = [o for o in order if o != 1] + [1]
    moves = []
    for h in range(PARTS):
        group_moves = []
        for o in order:
            peer = flip(me, o)
            group_moves.append(pltpu.make_async_remote_copy(
                src_ref=x_ref.at[:, pl.ds(pl.multiple_of(peer * width + h * part, part), part)],
                dst_ref=cols.at[mine, pl.ds(h * part, part)],
                send_sem=a2a_send.at[h, o],
                recv_sem=a2a_recv.at[h, o],
                device_id={"aux": peer}, device_id_type=MESH))
        moves.append(start(group_moves))

    for s, o in enumerate(steps):
        for copy in gather[s]:
            copy.wait_recv()
        owner = flip(me, o)
        if pair:
            pending.append(start(factor(1, s, half, owner, {"grp": twin})))
        pending.append(start(factor(2, s, half, owner, {"aux": mate})))
    if pair:
        for s, o in enumerate(steps):
            for copy in factor(1, s, other, flip(me, o), {"grp": twin}):
                copy.wait_recv()
            pending.append(start(factor(3, s, other, flip(me, o), {"aux": mate})))
    for s, o in enumerate(steps):
        for copy in factor(2, s, half, flip(mate, o), {"aux": mate}):
            copy.wait_recv()
        if pair:
            for copy in factor(3, s, other, flip(mate, o), {"aux": mate}):
                copy.wait_recv()
    for copy in own:
        copy.wait_recv()
    for copy in locals_[PARTS:]:
        copy.wait()

    for h in range(PARTS):
        locals_[h].wait()
        for copy in moves[h]:
            copy.wait_recv()
        here = pl.ds(h * part, part)
        for k in range(count):
            acc = cols[pl.ds(k * panel, panel), here].astype(jnp.float32)
            for j in range(k):
                acc = acc - jnp.dot(
                    low_all[k * (k - 1) // 2 + j],
                    out_ref[pl.ds(j * panel, panel), here],
                    preferred_element_type=jnp.float32)
            rest = acc.astype(jnp.bfloat16)
            out_ref[pl.ds(k * panel, panel), here] = jnp.dot(
                inv_all[k], rest, preferred_element_type=jnp.float32).astype(jnp.bfloat16)

    for copies in gather + [own] + moves + pending:
        for copy in copies:
            copy.wait_send()


def local(n, groups, integrals, inverses, lower_blocks):
    count, rows, panel = inverses.shape
    blocks = lower_blocks.shape[0]
    held = integrals.shape[0]
    width = integrals.shape[1] // n
    pair = groups % 2 == 0 and count % 2 == 0 and blocks % 2 == 0
    slots = max(n // 2 - 1, 1)
    return pl.pallas_call(
        functools.partial(kernel, n, pair),
        out_shape=jax.ShapeDtypeStruct((held * n, width), jnp.bfloat16),
        in_specs=[pl.BlockSpec(memory_space=pltpu.HBM)] * 3,
        out_specs=pl.BlockSpec(memory_space=pltpu.VMEM),
        scratch_shapes=[
            pltpu.VMEM((held * n, width), jnp.bfloat16),
            pltpu.VMEM((count, rows * n, panel), jnp.bfloat16),
            pltpu.VMEM((blocks, rows * n, panel), jnp.bfloat16),
            pltpu.SemaphoreType.DMA((PARTS, n)),
            pltpu.SemaphoreType.DMA((PARTS, n)),
            pltpu.SemaphoreType.DMA((4, slots, 2)),
            pltpu.SemaphoreType.DMA((4, slots, 2)),
            pltpu.SemaphoreType.DMA((2,)),
            pltpu.SemaphoreType.DMA((2,)),
            pltpu.SemaphoreType.DMA((PARTS + 2,)),
        ],
        compiler_params=pltpu.CompilerParams(collective_id=0, has_side_effects=True),
    )(integrals, inverses, lower_blocks)


def solution(mesh):
    placed = (P("aux", "grp"), P(None, "aux", None), P(None, "aux", None))
    body = functools.partial(local, mesh.shape["aux"], mesh.shape["grp"])
    return jax.shard_map(
        body, mesh=mesh, in_specs=placed, out_specs=P(None, ("grp", "aux")), check_vma=False
    )
```

time: 109 us -> 49.5 us (0.45)
  Pallas kernels: 0 us -> 46.3 us
  blocking collectives: 40 us -> 0 us
  waiting for transfers between devices: 26 us -> 0 us
  matrix products: 15.9 us -> 0 us
  between operations: 13.5 us -> 0.01 us
  local copies, waits for them, and re-layouts: 10.7 us -> 3.05 us
  other arithmetic: 2.73 us -> 0 us
    pallas_call x0 -> x1, Pallas kernels: none -> 46.3 us  [local(): pl.pallas_call(functools.partial(kernel, n, pair), out_shape=jax.ShapeDty...]
    all_to_all x1 -> x0, blocking collectives: 40 us -> none  [local(): lax.all_to_all(sectioned, 'aux', split_axis=1, concat_axis=0, tiled=True)]
    all_gather x2 -> x0, waiting for transfers between devices: 24.6 us -> none  [the longest x1 24.6 us: local(): lax.all_gather(lower_blocks, 'aux', axis=1, tiled=True)]
    dot_general x7 -> x0, matrix products: 15.9 us -> none  [the longest x4 10.3 us: local(): jnp.dot(inv_all[k], rest, preferred_element_type=jnp.float32)]
    convert_element_type x6 -> x0, local copies, waits for them, and re-layouts: 6.43 us -> none  [local(): acc = columns[k * panel:(k + 1) * panel].astype(jnp.float32)]
    concatenate x1 -> x0, other arithmetic: 1.46 us -> none  [local(): return jnp.concatenate(outs, axis=0)]
    unnamed x2 -> x0, waiting for transfers between devices: 1.41 us -> none
    convert_element_type x1 -> x0, other arithmetic: 1.27 us -> none  [local(): acc = columns[k * panel:(k + 1) * panel].astype(jnp.float32)]
  transfers between devices with their start and end apart: 2 -> 0, of which waited for: 1 -> 0; matrix products, arithmetic and copies ran while one was open for 13% -> 0% of each run, Pallas kernels for 0% -> 0%
where the time goes in v1:
time: 49.5 us; the launch traced here: 49.3 us
  Pallas kernels  46.3 us (94%)
  local copies, waits for them, and re-layouts  3.05 us (6%)
    pallas_call x1, Pallas kernels, local(): pl.pallas_call(functools.partial(kernel, n, pair), out_shape=jax.ShapeDty...  46.3 us
    unnamed x1, local copies, waits for them, and re-layouts  3.05 us

profile of v1, /device:TPU:0, one launch (start us, length us, event | category | flops | bytes accessed | tf_op | source)
XLA Modules:
  0.0 49.3 jit_solution(15870912699561841089)
XLA Ops:
  0.0 46.3 %shard_map.37 = bf16[2048,512]{1,0:T(8,128)(2,1)} custom-call(bf16[256,4096]{1,0:T(8,128)(2,1)} %x_ref.1, bf16[4,64,512]{2,1,0:T(8,128)(2,1)} %inv_ref.1, bf16[6,64,512]{2,1,0:T(8,128)(2,1)} %low_ref.1), custom_call_target="tpu_custom_call" | custom-call | tf_op jit(solution)/shard_map/pallas_call | solution.py:162
  46.3 3.0 %copy.5 = bf16[2048,512]{1,0:T(8,128)(2,1)} copy(bf16[2048,512]{1,0:T(8,128)(2,1)} %shard_map.37) | data formatting | bytes 4194304

commit v2 on v1

v2 whole, which is shorter than its diff:
```python
import functools

import jax
import jax.numpy as jnp
from jax import lax
from jax.experimental import pallas as pl
from jax.experimental.pallas import tpu as pltpu
from jax.sharding import PartitionSpec as P

MESH = pl.DeviceIdType.MESH
PARTS = 2


def flip(index, offset):
    result = 0
    bit = 1
    while bit <= offset or bit == 1:
        if offset & bit:
            result = result + bit * ((index // bit + 1) % 2)
        else:
            result = result + bit * ((index // bit) % 2)
        bit *= 2
    return result + (index // bit) * bit


def kernel(n, pair, colors, x_ref, inv_ref, low_ref, out_ref, cols, fac,
           a2a_send, a2a_recv, fac_send, fac_recv, own_send, own_recv, local_sem, fac_sem):
    me = lax.axis_index("aux")
    group = lax.axis_index("grp")
    held = x_ref.shape[0]
    width = out_ref.shape[1]
    part = width // PARTS
    count, rows, panel = inv_ref.shape
    total = fac.shape[0]
    slab = rows // colors
    mate = flip(me, 1)
    size = total // 2 if pair else total
    half = group % 2 if pair else 0
    other = (group + 1) % 2
    twin = flip(group, 1)

    def low_at(k, j):
        return k * (k + 1) // 2 + j

    def inv_at(k):
        return k * (k + 1) // 2 + k

    def at(device, color=None):
        if color is None:
            return pl.ds(pl.multiple_of(device * rows, rows), rows)
        return pl.ds(pl.multiple_of(device * rows + color * slab, slab), slab)

    fill = []
    for k in range(count):
        for j in range(k):
            fill.append((low_ref.at[k * (k - 1) // 2 + j], low_at(k, j)))
        fill.append((inv_ref.at[k], inv_at(k)))
    fill = [pltpu.make_async_copy(src, fac.at[i, at(me)], fac_sem.at[i]) for src, i in fill]
    for copy in fill:
        copy.start()
    mine = pl.ds(pl.multiple_of(me * held, held), held)
    locals_ = []
    for h in range(PARTS):
        locals_.append(pltpu.make_async_copy(
            x_ref.at[:, pl.ds(pl.multiple_of(me * width + h * part, part), part)],
            cols.at[mine, pl.ds(h * part, part)],
            local_sem.at[h]))
        locals_[h].start()

    barrier = pltpu.get_barrier_semaphore()
    for o in range(1, n):
        pl.semaphore_signal(barrier, inc=1, device_id={"aux": flip(me, o)}, device_id_type=MESH)
    if pair:
        pl.semaphore_signal(barrier, inc=1, device_id={"grp": twin}, device_id_type=MESH)
    for copy in fill:
        copy.wait()
    pl.semaphore_wait(barrier, n if pair else n - 1)

    def piece(kind, color, offset, which, owner, target):
        place = fac.at[pl.ds(which * size, size), at(owner, color)]
        return pltpu.make_async_remote_copy(
            src_ref=place, dst_ref=place,
            send_sem=fac_send.at[kind, color, offset // 2],
            recv_sem=fac_recv.at[kind, color, offset // 2],
            device_id=target, device_id_type=MESH)

    bits = [2 ** i for i in range(1, n.bit_length() - 1)]
    first, relays = [], []
    for step in range(len(bits)):
        for color in range(colors):
            order = bits if color == 0 else bits[::-1]
            first.append((color, 0, order[step]))
            reached = [0]
            for bit in order[:step]:
                reached += [o + bit for o in reached]
            relays += [(color, o, order[step]) for o in reached if o]

    started = []

    def start(copy):
        copy.start()
        started.append(copy)

    def send(color, offset, bit):
        start(piece(0, color, offset ^ bit, half, flip(me, offset), {"aux": flip(me, bit)}))

    for hop in first:
        send(*hop)
    own = pltpu.make_async_remote_copy(
        src_ref=fac.at[:, at(me)], dst_ref=fac.at[:, at(me)],
        send_sem=own_send.at[0], recv_sem=own_recv.at[0],
        device_id={"aux": mate}, device_id_type=MESH)
    start(own)

    seen = []

    def arrived(color, offset):
        if (color, offset) in seen:
            return
        seen.append((color, offset))
        owner = flip(me, offset)
        piece(0, color, offset, half, owner, {"aux": mate}).wait_recv()
        for c, o, bit in relays:
            if (c, o) == (color, offset):
                send(c, o, bit)
        if pair:
            start(piece(1, color, offset, half, owner, {"grp": twin}))
        start(piece(2, color, offset, half, owner, {"aux": mate}))

    for color, offset, _ in relays:
        arrived(color, offset)

    order = [o for o in range(n - 1, 0, -1)]
    order = [o for o in order if o % 2 == 0] + [o for o in order if o % 2]
    moves = []
    for h in range(PARTS):
        moves.append([])
        for o in order:
            peer = flip(me, o)
            copy = pltpu.make_async_remote_copy(
                src_ref=x_ref.at[:, pl.ds(pl.multiple_of(peer * width + h * part, part), part)],
                dst_ref=cols.at[mine, pl.ds(h * part, part)],
                send_sem=a2a_send.at[h, o],
                recv_sem=a2a_recv.at[h, o],
                device_id={"aux": peer}, device_id_type=MESH)
            moves[h].append(copy)
            start(copy)

    for color, offset, bit in first + relays:
        arrived(color, offset ^ bit)
    if pair:
        for color, offset in seen:
            owner = flip(me, offset)
            piece(1, color, offset, other, owner, {"grp": twin}).wait_recv()
            start(piece(3, color, offset, other, owner, {"aux": mate}))
    for color, offset in seen:
        owner = flip(mate, offset)
        piece(2, color, offset, half, owner, {"aux": mate}).wait_recv()
        if pair:
            piece(3, color, offset, other, owner, {"aux": mate}).wait_recv()
    own.wait_recv()

    for h in range(PARTS):
        locals_[h].wait()
        for copy in moves[h]:
            copy.wait_recv()
        here = pl.ds(h * part, part)
        for k in range(count):
            acc = cols[pl.ds(k * panel, panel), here].astype(jnp.float32)
            for j in range(k):
                acc = acc - jnp.dot(
                    fac[low_at(k, j)], out_ref[pl.ds(j * panel, panel), here],
                    preferred_element_type=jnp.float32)
            rest = acc.astype(jnp.bfloat16)
            out_ref[pl.ds(k * panel, panel), here] = jnp.dot(
                fac[inv_at(k)], rest, preferred_element_type=jnp.float32).astype(jnp.bfloat16)

    for copy in started:
        copy.wait_send()


def local(n, groups, integrals, inverses, lower_blocks):
    count, rows, panel = inverses.shape
    blocks = count + lower_blocks.shape[0]
    held = integrals.shape[0]
    width = integrals.shape[1] // n
    pair = groups % 2 == 0 and blocks % 2 == 0
    colors = 2 if rows % 32 == 0 else 1
    slots = max(n // 2, 1)
    return pl.pallas_call(
        functools.partial(kernel, n, pair, colors),
        out_shape=pltpu.VMEM((held * n, width), jnp.bfloat16),
        in_specs=[pl.BlockSpec(memory_space=pltpu.HBM)] * 3,
        out_specs=pl.BlockSpec(memory_space=pltpu.VMEM),
        scratch_shapes=[
            pltpu.VMEM((held * n, width), jnp.bfloat16),
            pltpu.VMEM((blocks, rows * n, panel), jnp.bfloat16),
            pltpu.SemaphoreType.DMA((PARTS, n)),
            pltpu.SemaphoreType.DMA((PARTS, n)),
            pltpu.SemaphoreType.DMA((4, colors, slots)),
            pltpu.SemaphoreType.DMA((4, colors, slots)),
            pltpu.SemaphoreType.DMA((1,)),
            pltpu.SemaphoreType.DMA((1,)),
            pltpu.SemaphoreType.DMA((PARTS,)),
            pltpu.SemaphoreType.DMA((blocks,)),
        ],
        compiler_params=pltpu.CompilerParams(
            collective_id=0, has_side_effects=True, vmem_limit_bytes=32 * 2**20),
    )(*(pltpu.with_memory_space_constraint(a, pltpu.HBM) for a in (integrals, inverses, lower_blocks)))


def solution(mesh):
    placed = (P("aux", "grp"), P(None, "aux", None), P(None, "aux", None))
    body = functools.partial(local, mesh.shape["aux"], mesh.shape["grp"])
    return jax.shard_map(
        body, mesh=mesh, in_specs=placed, out_specs=P(None, ("grp", "aux")), check_vma=False
    )
```

time: 49.5 us -> 42.9 us (0.87)
  Pallas kernels: 46.3 us -> 41.4 us
  local copies, waits for them, and re-layouts: 3.05 us -> 1.32 us
    pallas_call x1, Pallas kernels: 46.3 us -> 41.4 us  [local(): pl.pallas_call(functools.partial(kernel, n, pair, colors), out_shape=pltp...]
    unnamed x1, local copies, waits for them, and re-layouts: 3.05 us -> 1.32 us
where the time goes in v2:
time: 42.9 us; the launch traced here: 42.8 us
  Pallas kernels  41.4 us (97%)
  local copies, waits for them, and re-layouts  1.32 us (3%)
    pallas_call x1, Pallas kernels, local(): pl.pallas_call(functools.partial(kernel, n, pair, colors), out_shape=pltp...  41.4 us
    unnamed x1, local copies, waits for them, and re-layouts  1.32 us

profile of v2, /device:TPU:0, one launch (start us, length us, event | category | flops | bytes accessed | tf_op | source)
XLA Modules:
  0.0 42.8 jit_solution(1509528665760473057)
XLA Ops:
  0.0 41.4 %shard_map.37 = bf16[2048,512]{1,0:T(8,128)(2,1)S(1)} custom-call(bf16[256,4096]{1,0:T(8,128)(2,1)} %x_ref.1, bf16[4,64,512]{2,1,0:T(8,128)(2,1)} %inv_ref.1, bf16[6,64,512]{2,1,0:T(8,128)(2,1)} %low_ref.1), custom_call_target="tpu_custom_call" | custom-call | tf_op jit(solution)/shard_map/pallas_call | solution.py:190
  41.4 1.3 %copy.5 = bf16[2048,512]{1,0:T(8,128)(2,1)} copy(bf16[2048,512]{1,0:T(8,128)(2,1)S(1)} %shard_map.37) | data formatting | bytes 4194304
